TPU v7x, 256 devices: a whole 4x4x8 slice. The times are simulated.
256 devices in a mesh: frame: 64 (over y, z, core), text: 4 (over x).
Axes of the slice: x: 4, y: 4, z: 8, core: 2. Of those that a mesh axis runs over, the one named last changes fastest.
Arguments:
- frame_keys: bfloat16 [32768, 4096], P('frame', 'text'), may hold values from -6 to 6
- frame_values: bfloat16 [32768, 4096], P('frame', 'text'), may hold values from -6 to 6
- frame_grads: bfloat16 [32768, 4096], P('frame', 'text'), may hold values from -6 to 6
- text_keys: bfloat16 [8192, 4096], P(('frame', 'text')), may hold values from -6 to 6
- text_values: bfloat16 [8192, 4096], P(('frame', 'text')), may hold values from -6 to 6
- text_grads: bfloat16 [8192, 4096], P(('frame', 'text')), may hold values from -6 to 6
- band_first: int32 [256], P('frame'), may hold values from 0 to 63, as said below
- band_count: int32 [256], P('frame'), may hold values from 1 to 3
Outputs:
- frame_out: bfloat16 [32768, 4096], P('frame', 'text')
- text_out: bfloat16 [8192, 4096], P('frame', 'text')
- frame_key_grad: bfloat16 [32768, 4096], P('frame', 'text')
- frame_value_grad: bfloat16 [32768, 4096], P('frame', 'text')
- text_key_grad: bfloat16 [8192, 4096], P('frame', 'text')
- text_value_grad: bfloat16 [8192, 4096], P('frame', 'text')
Inputs may be any that keep to these rules, and one draw needn't show every extreme that they name: For frame block b, band_first[b] is b // 4 - 1 or b // 4, and band_first[b] + band_count[b] - 1 is b // 4 or b // 4 + 1, so every text block lies in some band.
All inputs are finite; a program needn't handle non-finite values.
Results may differ from a plain program's by a relative error of at most 0.023.
Values may be sent and summed in bfloat16 or wider, within the bound.
A program may use at most 128 MiB of HBM per device.

v0:
```python
import functools
import math
import jax
import jax.numpy as jnp
from jax import lax
from jax.sharding import PartitionSpec as P

HEAD_DIM = 128
BLOCK = 128
NEGATIVE = -1e30


def extended(array, sides, width):
    for axis, dim in sides:
        size, length = (lax.axis_size(axis), array.shape[dim])
        up = [(i, (i + 1) % size) for i in range(size - 1)]
        down = [(j, i) for i, j in up]
        last = lax.slice_in_dim(array, length - width, length, axis=dim)
        initial = lax.slice_in_dim(array, 0, width, axis=dim)
        before = lax.ppermute(last, axis, up)
        after = lax.ppermute(initial, axis, down)
        array = jnp.concatenate([before, array, after], axis=dim)
    return array


def from_behind(block, axis, distance):
    devices = range(lax.axis_size(axis))
    route = [(i - distance, i) for i in devices if i - distance in devices]
    return lax.ppermute(block, axis, route)


def block_mask(first_ids, count_ids, text_ids):
    lower = first_ids[:, None]
    upper = lower + count_ids[:, None]
    inside = (text_ids[None, :] >= lower) & (text_ids[None, :] < upper)
    row_blocks, col_blocks = inside.shape
    grown = jnp.broadcast_to(inside[:, None, :, None], (row_blocks, BLOCK, col_blocks, BLOCK))
    return grown.reshape(row_blocks * BLOCK, col_blocks * BLOCK)


def on_device(
    frame_keys,
    frame_values,
    frame_grads,
    text_keys,
    text_values,
    text_grads,
    band_first,
    band_count,
):
    score_scale = 1.0 / math.sqrt(HEAD_DIM)
    stacked = jnp.stack([text_keys, text_values, text_grads])
    group_count = lax.axis_size("text")
    rows_sub = stacked.shape[1]
    window = extended(stacked, (("frame", 1),), rows_sub)
    arrived = lax.all_to_all(window, "text", split_axis=2, concat_axis=1, tiled=True)
    head_width = arrived.shape[2]
    arrived = arrived.reshape(3, group_count, 3, rows_sub, head_width).transpose(0, 2, 1, 3, 4)
    own_rows = group_count * rows_sub
    arrived = arrived.reshape(3, 3 * own_rows, head_width)
    own_text = arrived[:, own_rows : 2 * own_rows]
    head_count = frame_keys.shape[1] // HEAD_DIM
    frame_rows = frame_keys.shape[0]
    win_rows = 3 * own_rows
    keys_win = arrived[0].reshape(win_rows, head_count, HEAD_DIM)
    values_win = arrived[1].reshape(win_rows, head_count, HEAD_DIM)
    grads_win = arrived[2].reshape(win_rows, head_count, HEAD_DIM)
    own_grads_text = own_text[2].reshape(own_rows, head_count, HEAD_DIM)
    frame_k = frame_keys.reshape(frame_rows, head_count, HEAD_DIM)
    frame_v = frame_values.reshape(frame_rows, head_count, HEAD_DIM)
    frame_g = frame_grads.reshape(frame_rows, head_count, HEAD_DIM)
    frame_index = lax.axis_index("frame")
    text_per_dev = own_rows // BLOCK
    text_ids = (frame_index - 1) * text_per_dev + jnp.arange(3 * text_per_dev, dtype=jnp.int32)
    live_pairs = block_mask(band_first, band_count, text_ids)[None]
    scores = score_scale * jnp.einsum(
        "fhd,thd->hft", frame_k, keys_win, preferred_element_type=jnp.float32
    )
    row_max = jnp.max(jnp.where(live_pairs, scores, NEGATIVE), axis=2)
    row_exp = jnp.exp(jnp.where(live_pairs, scores - row_max[:, :, None], NEGATIVE))
    row_total = jnp.sum(row_exp, axis=2)
    row_probs = row_exp / row_total[:, :, None]
    row_low = row_probs.astype(jnp.bfloat16)
    frame_out = jnp.einsum(
        "hft,thd->fhd", row_low, values_win, preferred_element_type=jnp.float32
    ).astype(jnp.bfloat16)
    frame_dot = jnp.sum(frame_g.astype(jnp.float32) * frame_out.astype(jnp.float32), axis=2).T
    col_max = jnp.max(jnp.where(live_pairs, scores, NEGATIVE), axis=1)
    col_exp = jnp.exp(jnp.where(live_pairs, scores - col_max[:, None, :], NEGATIVE))
    col_total = jnp.sum(col_exp, axis=1)
    col_weights = col_exp.astype(jnp.bfloat16)
    col_sum = jnp.einsum("hft,fhd->thd", col_weights, frame_v, preferred_element_type=jnp.float32)
    own_slice = slice(own_rows, 2 * own_rows)
    members = [(col_max[:, own_slice], col_total[:, own_slice], col_sum[own_slice])]
    for offset, segment in ((-1, 0), (1, 2)):
        window_slice = slice(segment * own_rows, (segment + 1) * own_rows)
        members.append(
            from_behind(
                (col_max[:, window_slice], col_total[:, window_slice], col_sum[window_slice]),
                "frame",
                offset,
            )
        )
    safe_max = [jnp.where(member[1] > 0, member[0], NEGATIVE) for member in members]
    column_peak = functools.reduce(jnp.maximum, safe_max)
    factors = [jnp.exp(partial_max - column_peak) for partial_max in safe_max]
    column_total = functools.reduce(
        jnp.add, [member[1] * factor for member, factor in zip(members, factors)]
    )
    column_sum = functools.reduce(
        jnp.add, [member[2] * factor.T[:, :, None] for member, factor in zip(members, factors)]
    )
    text_out = (column_sum / column_total.T[:, :, None]).astype(jnp.bfloat16)
    text_dot = jnp.sum(own_grads_text.astype(jnp.float32) * text_out.astype(jnp.float32), axis=2).T
    stats_win = (
        extended(column_peak, (("frame", 1),), own_rows),
        extended(column_total, (("frame", 1),), own_rows),
        extended(text_dot, (("frame", 1),), own_rows),
    )
    win_max, win_total, win_dot = stats_win
    win_total = jnp.where(win_total > 0, win_total, 1.0)
    col_probs = (
        jnp.exp(jnp.where(live_pairs, scores - win_max[:, None, :], NEGATIVE))
        / win_total[:, None, :]
    )
    grad_rows = jnp.einsum("fhd,thd->hft", frame_g, values_win, preferred_element_type=jnp.float32)
    grad_cols = jnp.einsum("fhd,thd->hft", frame_v, grads_win, preferred_element_type=jnp.float32)
    grad_score = (
        row_probs * (grad_rows - frame_dot[:, :, None])
        + col_probs * (grad_cols - win_dot[:, None, :])
    ).astype(jnp.bfloat16)
    frame_key_grad = (
        score_scale
        * jnp.einsum("hft,thd->fhd", grad_score, keys_win, preferred_element_type=jnp.float32)
    ).astype(jnp.bfloat16)
    frame_value_grad = jnp.einsum(
        "hft,thd->fhd",
        col_probs.astype(jnp.bfloat16),
        grads_win,
        preferred_element_type=jnp.float32,
    ).astype(jnp.bfloat16)
    key_terms = score_scale * jnp.einsum(
        "hft,fhd->thd", grad_score, frame_k, preferred_element_type=jnp.float32
    )
    value_terms = jnp.einsum("hft,fhd->thd", row_low, frame_g, preferred_element_type=jnp.float32)
    key_total = key_terms[own_slice]
    value_total = value_terms[own_slice]
    for offset, segment in ((-1, 0), (1, 2)):
        window_slice = slice(segment * own_rows, (segment + 1) * own_rows)
        returned = (
            from_behind(key_terms[window_slice].astype(jnp.bfloat16), "frame", offset).astype(
                jnp.float32
            ),
            from_behind(value_terms[window_slice].astype(jnp.bfloat16), "frame", offset).astype(
                jnp.float32
            ),
        )
        key_total = key_total + returned[0]
        value_total = value_total + returned[1]
    out_width = head_count * HEAD_DIM
    return (
        frame_out.reshape(frame_rows, out_width),
        text_out.reshape(own_rows, out_width),
        frame_key_grad.reshape(frame_rows, out_width),
        frame_value_grad.reshape(frame_rows, out_width),
        key_total.astype(jnp.bfloat16).reshape(own_rows, out_width),
        value_total.astype(jnp.bfloat16).reshape(own_rows, out_width),
    )


def solution(mesh):
    in_specs = (
        P("frame", "text"),
        P("frame", "text"),
        P("frame", "text"),
        P(("frame", "text"), None),
        P(("frame", "text"), None),
        P(("frame", "text"), None),
        P("frame"),
        P("frame"),
    )
    out_specs = (
        P("frame", "text"),
        P("frame", "text"),
        P("frame", "text"),
        P("frame", "text"),
        P("frame", "text"),
        P("frame", "text"),
    )
    return jax.shard_map(
        on_device, mesh=mesh, in_specs=in_specs, out_specs=out_specs, check_vma=False
    )
```

profile of v0, /device:TPU:24, one launch (start us, length us, event | category | flops | bytes accessed | tf_op | source)
XLA Modules:
  0.0 224.5 jit_solution(12583766159716517799)
XLA Ops:
  1.9 7.4 %collective-permute-start.1 = (bf16[3,32,4096]{2,1,0:T(8,128)(2,1)S(1)}, bf16[3,32,4096]{2,1,0:T(8,128)(2,1)S(1)}, u32[]{:S(2)}, u32[]{:S(2)}) collective-permute-start(bf16[3,32,4096]{2,1,0:T(8,128)(2,1)S(1)} %pad_maximum_fusion.1), channel_id=1, source_target_pairs={{4,0},{8,4},{12,8},{16,12},{20,16},{24,20},{28,24},{32,28},{36,32}... | collective-permute-start | bytes 2359304 | tf_op jit(solution)/shard_map/ppermute | solution.py:21
  9.3 1.9 collective-permute-start
  11.3 7.6 %collective-permute-done.1 = bf16[3,32,4096]{2,1,0:T(8,128)(2,1)S(1)} collective-permute-done((bf16[3,32,4096]{2,1,0:T(8,128)(2,1)S(1)}, bf16[3,32,4096]{2,1,0:T(8,128)(2,1)S(1)}, u32[]{:S(2)}, u32[]{:S(2)}) %collective-permute-start.1) | collective-permute-done | bytes 786464 | tf_op jit(solution)/shard_map/ppermute | solution.py:21
  18.8 5.9 %collective-permute-done = bf16[3,32,4096]{2,1,0:T(8,128)(2,1)S(1)} collective-permute-done((bf16[3,32,4096]{2,1,0:T(8,128)(2,1)S(1)}, bf16[3,32,4096]{2,1,0:T(8,128)(2,1)S(1)}, u32[]{:S(2)}, u32[]{:S(2)}) %collective-permute-start) | collective-permute-done | bytes 786464 | tf_op jit(solution)/shard_map/ppermute | solution.py:20
  24.7 1.3 pad_maximum_fusion
  26.1 4.8 %copy.128 = bf16[3,96,4096]{1,0,2:T(4,128)(2,1)} copy(bf16[3,96,4096]{2,1,0:T(8,128)(2,1)S(1)} %pad_maximum_fusion) | data formatting | bytes 4718592 | tf_op jit(solution)/shard_map/concatenate | solution.py:22
  30.9 5.0 %all-to-all-start = ((bf16[3,96,4096]{1,0,2:T(4,128)(2,1)}), bf16[3,96,4096]{1,0,2:T(4,128)(2,1)}, u32[]{:S(2)}, u32[]{:S(2)}) async-start(bf16[3,96,4096]{1,0,2:T(4,128)(2,1)} %copy.128), calls=%async_computation | async-start | bytes 8388608 | tf_op jit(solution)/shard_map/all_to_all | solution.py:56
  37.0 1.3 copy.139
  38.3 1.3 copy.169
  39.6 37.6 %all-to-all-done = bf16[3,96,4096]{1,0,2:T(4,128)(2,1)} async-done(((bf16[3,96,4096]{1,0,2:T(4,128)(2,1)}), bf16[3,96,4096]{1,0,2:T(4,128)(2,1)}, u32[]{:S(2)}, u32[]{:S(2)}) %all-to-all-start) | async-done | bytes 2359328 | tf_op jit(solution)/shard_map/all_to_all | solution.py:56
  77.2 5.5 %copy.130 = bf16[3,4,96,1024]{3,2,1,0:T(8,128)(2,1)S(1)} copy(bf16[3,4,96,1024]{2,0,3,1:T(4,128)(2,1)} %bitcast.5) | data formatting | bytes 4718592 | tf_op jit(solution)/shard_map/all_to_all | solution.py:56
  82.6 1.7 copy.145
  84.3 1.4 fusion.61
  86.9 1.6 copy.147
  88.5 5.5 %fusion.10 = (f32[8,384]{1,0:T(8,128)S(1)}, f32[8,384,512]{2,1,0:T(8,128)}) fusion(pred[512,384]{0,1:T(8,128)(4,1)} %bitcast.162, bf16[384,8,128]{0,2,1:T(8,128)(2,1)S(1)} %copy.147, bf16[512,8,128]{0,2,1:T(8,128)(2,1)} %bitcast.144), kind=kOutput, calls=%fused_computation.16 | convolution fusion | flops 407368704 | bytes 8335360 | tf_op jit(solution)/shard_map/fhd,thd->hft/dot_general | solution.py:76
  94.0 5.8 %fusion.67 = (f32[8,512]{1,0:T(8,128)S(1)}, f32[8,512,384]{1,2,0:T(8,128)}) fusion(pred[512,384]{0,1:T(8,128)(4,1)S(1)} %bitcast.164, bf16[384,8,128]{0,2,1:T(8,128)(2,1)S(1)} %copy.147, bf16[512,8,128]{0,2,1:T(8,128)(2,1)S(1)} %bitcast.145), kind=kOutput, calls=%fused_computation.92 | convolution fusion | flops 814743936 | bytes 8339456 | tf_op jit(solution)/shard_map/sub | solution.py:80
  99.8 1.3 copy.142
  102.2 2.4 %copy.149 = bf16[384,8,128]{0,2,1:T(8,128)(2,1)} copy(bf16[384,8,128]{2,1,0:T(8,128)(2,1)} %bitcast.156) | data formatting | bytes 1572864 | tf_op jit(solution)/shard_map/reshape;squeeze | solution.py:67
  106.0 4.3 %fusion.12 = f32[8,384]{1,0:T(8,128)S(1)} fusion(f32[8,384,512]{2,1,0:T(8,128)} %get-tuple-element.59, f32[8,384]{1,0:T(8,128)S(1)} %get-tuple-element.58, pred[512,384]{0,1:T(8,128)(4,1)S(1)} %bitcast.165), kind=kLoop, calls=%fused_computation.18 | loop fusion | flops 6288384 | bytes 6512640 | tf_op jit(solution)/shard_map/reduce_sum | solution.py:90
  110.4 2.0 fusion.30
  112.4 3.6 %fusion.34 = f32[8,384,512]{2,1,0:T(8,128)} fusion(bf16[384,8,128]{0,2,1:T(8,128)(2,1)S(1)} %copy-done.9, bf16[512,1024]{1,0:T(8,128)(2,1)S(1)} %copy-done), kind=kOutput, calls=%fused_computation.42 | convolution fusion | flops 402653184 | bytes 8126464 | tf_op jit(solution)/shard_map/fhd,thd->hft/dot_general | solution.py:127
  116.0 9.2 %collective-permute-start.2 = (f32[8,128]{1,0:T(8,128)S(1)}, f32[8,128]{1,0:T(8,128)S(1)}, u32[]{:S(2)}, u32[]{:S(2)}) collective-permute-start(f32[8,128]{1,0:T(8,128)S(1)} %get-tuple-element.54), channel_id=1, source_target_pairs={{4,0},{8,4},{12,8},{16,12},{20,16},{24,20},{28,24},{32,28},{36,32}... | collective-permute-start | bytes 12296 | tf_op jit(solution)/shard_map/ppermute | solution.py:29
  125.3 1.9 collective-permute-start.4
  127.2 5.8 %collective-permute-start.3 = (f32[8,128]{1,0:T(8,128)S(1)}, f32[8,128]{1,0:T(8,128)S(1)}, u32[]{:S(2)}, u32[]{:S(2)}) collective-permute-start(f32[8,128]{1,0:T(8,128)S(1)} %get-tuple-element.52), channel_id=1, source_target_pairs={{4,0},{8,4},{12,8},{16,12},{20,16},{24,20},{28,24},{32,28},{36,32}... | collective-permute-start | bytes 12296 | tf_op jit(solution)/shard_map/ppermute | solution.py:29
  132.9 1.9 collective-permute-start.5
  135.9 5.9 %collective-permute-start.6 = (f32[128,8,128]{0,2,1:T(8,128)}, f32[128,8,128]{0,2,1:T(8,128)}, u32[]{:S(2)}, u32[]{:S(2)}) collective-permute-start(f32[128,8,128]{0,2,1:T(8,128)} %get-tuple-element.43), channel_id=1, source_target_pairs={{4,0},{8,4},{12,8},{16,12},{20,16},{24,20},{28,24},{32,28},{36,32}... | collective-permute-start | bytes 1572872 | tf_op jit(solution)/shard_map/ppermute | solution.py:29
  143.7 2.2 fusion.69
  146.9 1.9 collective-permute-start.7
  148.9 5.8 %collective-permute-start.11 = (f32[8,128]{1,0:T(8,128)S(1)}, f32[8,128]{1,0:T(8,128)S(1)}, u32[]{:S(2)}, u32[]{:S(2)}) collective-permute-start(f32[8,128]{1,0:T(8,128)S(1)} %get-tuple-element.50), channel_id=1, source_target_pairs={{4,0},{8,4},{12,8},{16,12},{20,16},{24,20},{28,24},{32,28},{36,32}... | collective-permute-start | bytes 12296 | tf_op jit(solution)/shard_map/ppermute | solution.py:21
  154.7 1.9 collective-permute-start.10
  158.6 1.3 copy.154
  159.9 5.7 %collective-permute-start.16 = (bf16[128,8,128]{0,2,1:T(8,128)(2,1)}, bf16[128,8,128]{0,2,1:T(8,128)(2,1)}, u32[]{:S(2)}, u32[]{:S(2)}) collective-permute-start(bf16[128,8,128]{0,2,1:T(8,128)(2,1)} %get-tuple-element.45), channel_id=1, source_target_pairs={{4,0},{8,4},{12,8},{16,12},{20,16},{24,20},{28,24},{32,28},{36,32}... | collective-permute-start | bytes 786440 | tf_op jit(solution)/shard_map/ppermute | solution.py:29
  165.6 1.9 collective-permute-start.8
  167.6 5.8 %collective-permute-start.9 = (f32[8,128]{1,0:T(8,128)S(1)}, f32[8,128]{1,0:T(8,128)S(1)}, u32[]{:S(2)}, u32[]{:S(2)}) collective-permute-start(f32[8,128]{1,0:T(8,128)S(1)} %get-tuple-element.39), channel_id=1, source_target_pairs={{4,0},{8,4},{12,8},{16,12},{20,16},{24,20},{28,24},{32,28},{36,32}... | collective-permute-start | bytes 12296 | tf_op jit(solution)/shard_map/ppermute | solution.py:21
  173.3 1.9 collective-permute-start.17
  175.3 6.3 %fusion.27 = bf16[8,128,512]{2,1,0:T(8,128)(2,1)} fusion(bf16[384,8,128]{0,2,1:T(8,128)(2,1)S(1)} %copy-done.10, f32[8,384,512]{2,1,0:T(8,128)} %get-tuple-element.59, f32[8,384]{1,0:T(8,128)S(1)} %compare_select_fusion, f32[8,384]{1,0:T(8,128)S(1)} %pad_maximum_fusion.2, pred[512,384]{0,1:T(8,128)(4,1)} %bitcast.163), kind=kOutput, calls=%fused_computation.37 | convolution fusion | flops 411041792 | bytes 8347648 | tf_op jit(solution)/shard_map/hft,thd->fhd/dot_general | solution.py:136
  181.6 2.3 %copy.157 = bf16[512,1024]{1,0:T(8,128)(2,1)} copy(bf16[512,1024]{0,1:T(8,128)(2,1)} %bitcast.171) | data formatting | bytes 2097152
  184.0 1.6 multiply_reduce_fusion.1
  185.6 5.8 %collective-permute-start.13 = (f32[8,128]{1,0:T(8,128)S(1)}, f32[8,128]{1,0:T(8,128)S(1)}, u32[]{:S(2)}, u32[]{:S(2)}) collective-permute-start(f32[8,128]{1,0:T(8,128)S(1)} %bitcast.181), channel_id=1, source_target_pairs={{4,0},{8,4},{12,8},{16,12},{20,16},{24,20},{28,24},{32,28},{36,32}... | collective-permute-start | bytes 12296 | tf_op jit(solution)/shard_map/ppermute | solution.py:21
  191.3 1.9 collective-permute-start.12
  193.3 1.3 fusion.42
  196.3 2.1 collective-permute-done.12
  198.4 8.2 %fusion.2 = bf16[8,512,384]{1,2,0:T(8,128)(2,1)S(1)} fusion(f32[8,384,512]{2,1,0:T(8,128)} %fusion.34, f32[8,384]{1,0:T(8,128)S(1)} %pad_maximum_fusion.3, f32[8,512]{1,0:T(8,128)S(1)} %bitcast.180, bf16[512,8,128]{0,2,1:T(8,128)(2,1)S(1)} %bitcast.148, f32[8,512,384]{1,2,0:T(8,128)} %get-tuple-element.57, f32[8,512]{1,0:T(8,128)S(1)} %get-tuple-element.56, ...), kind=kOutput, calls=%fused_computation.3 | convolution fusion | flops 419954688 | bytes 24121344 | tf_op jit(solution)/shard_map/fhd,thd->hft/dot_general | solution.py:126
  206.7 2.2 fusion.68
  209.0 3.7 %collective-permute-start.14 = (bf16[128,8,128]{0,2,1:T(8,128)(2,1)S(1)}, bf16[128,8,128]{0,2,1:T(8,128)(2,1)S(1)}, u32[]{:S(2)}, u32[]{:S(2)}) collective-permute-start(bf16[128,8,128]{0,2,1:T(8,128)(2,1)S(1)} %get-tuple-element.47), channel_id=1, source_target_pairs={{4,0},{8,4},{12,8},{16,12},{20,16},{24,20},{28,24},{32,28},{36,32}... | collective-permute-start | bytes 786440 | tf_op jit(solution)/shard_map/ppermute | solution.py:29
  212.7 1.9 collective-permute-start.15
  215.4 1.3 copy.156
  216.7 5.8 %collective-permute-done.15 = bf16[128,8,128]{0,2,1:T(8,128)(2,1)S(1)} collective-permute-done((bf16[128,8,128]{0,2,1:T(8,128)(2,1)S(1)}, bf16[128,8,128]{0,2,1:T(8,128)(2,1)S(1)}, u32[]{:S(2)}, u32[]{:S(2)}) %collective-permute-start.15) | collective-permute-done | bytes 262176 | tf_op jit(solution)/shard_map/ppermute | solution.py:29
  (92 shorter events, 16.4 us)
Async XLA Ops:
  0.6 109.7 %copy-start = (bf16[512,1024]{1,0:T(8,128)(2,1)S(1)}, bf16[512,1024]{1,0:T(8,128)(2,1)}, u32[]{:S(2)}) copy-start(bf16[512,1024]{1,0:T(8,128)(2,1)} %param.9) | copy-start | bytes 3145732
  1.9 16.9 %collective-permute-start.1 = (bf16[3,32,4096]{2,1,0:T(8,128)(2,1)S(1)}, bf16[3,32,4096]{2,1,0:T(8,128)(2,1)S(1)}, u32[]{:S(2)}, u32[]{:S(2)}) collective-permute-start(bf16[3,32,4096]{2,1,0:T(8,128)(2,1)S(1)} %pad_maximum_fusion.1), channel_id=1, source_target_pairs={{4,0},{8,4},{12,8},{16,12},{20,16},{24,20},{28,24},{32,28},{36,32}... | collective-permute-start | bytes 2359304 | tf_op jit(solution)/shard_map/ppermute | solution.py:21
  9.3 15.4 %collective-permute-start = (bf16[3,32,4096]{2,1,0:T(8,128)(2,1)S(1)}, bf16[3,32,4096]{2,1,0:T(8,128)(2,1)S(1)}, u32[]{:S(2)}, u32[]{:S(2)}) collective-permute-start(bf16[3,32,4096]{2,1,0:T(8,128)(2,1)S(1)} %pad_maximum_fusion.1), channel_id=1, source_target_pairs={{0,4},{4,8},{8,12},{12,16},{16,20},{20,24},{24,28},{28,32},{32,36}... | collective-permute-start | bytes 2359304 | tf_op jit(solution)/shard_map/ppermute | solution.py:20
  26.1 9.8 %copy-start.17 = (s32[4]{0:T(128)S(1)}, s32[4]{0:T(128)}, u32[]{:S(2)}) copy-start(s32[4]{0:T(128)} %param.14) | copy-start | bytes 52
  26.1 9.8 %copy-start.18 = (s32[4]{0:T(128)S(1)}, s32[4]{0:T(128)}, u32[]{:S(2)}) copy-start(s32[4]{0:T(128)} %param.15) | copy-start | bytes 52
  30.9 6.1 %copy-start.15 = (bf16[512,1024]{1,0:T(8,128)(2,1)S(1)}, bf16[512,1024]{1,0:T(8,128)(2,1)}, u32[]{:S(2)}) copy-start(bf16[512,1024]{1,0:T(8,128)(2,1)} %param.10) | copy-start | bytes 3145732
  30.9 7.4 %copy-start.16 = (bf16[512,1024]{1,0:T(8,128)(2,1)S(1)}, bf16[512,1024]{1,0:T(8,128)(2,1)}, u32[]{:S(2)}) copy-start(bf16[512,1024]{1,0:T(8,128)(2,1)} %param.8) | copy-start | bytes 3145732
  30.9 46.3 %all-to-all-start = ((bf16[3,96,4096]{1,0,2:T(4,128)(2,1)}), bf16[3,96,4096]{1,0,2:T(4,128)(2,1)}, u32[]{:S(2)}, u32[]{:S(2)}) async-start(bf16[3,96,4096]{1,0,2:T(4,128)(2,1)} %copy.128), calls=%async_computation | async-start | bytes 8388608 | tf_op jit(solution)/shard_map/all_to_all | solution.py:56
  85.7 8.3 %copy-start.2 = (bf16[512,1024]{0,1:T(8,128)(2,1)S(1)}, bf16[512,1024]{0,1:T(8,128)(2,1)}, u32[]{:S(2)}) copy-start(bf16[512,1024]{0,1:T(8,128)(2,1)} %copy.169) | copy-start | bytes 3145732
  85.7 8.3 %copy-start.12 = (pred[48,8,4,128]{3,1,2,0:T(8,128)(4,1)S(1)}, pred[48,8,4,128]{3,1,2,0:T(8,128)(4,1)}, u32[]{:S(2)}) copy-start(pred[48,8,4,128]{3,1,2,0:T(8,128)(4,1)} %copy.190) | copy-start | bytes 589828
  88.5 11.3 %copy-start.5 = (bf16[384,8,128]{0,2,1:T(8,128)(2,1)}, bf16[384,8,128]{0,2,1:T(8,128)(2,1)S(1)}, u32[]{:S(2)}) copy-start(bf16[384,8,128]{0,2,1:T(8,128)(2,1)S(1)} %copy.147) | copy-start | bytes 2359300
  99.8 10.6 %slice-start = ((s8[6291456]{0:T(1024)(128)(4,1)}), s8[2097152]{0:T(1024)(128)(4,1)S(1)}, s32[]{:S(2)}) async-start(s8[6291456]{0:T(1024)(128)(4,1)} %bitcast.140), calls=%async_computation.1 | async-start | bytes 4194304
  105.8 4.6 %slice-start.1 = ((s8[6291456]{0:T(1024)(128)(4,1)}), s8[4194304]{0:T(1024)(128)(4,1)S(1)}, s32[]{:S(2)}) async-start(s8[6291456]{0:T(1024)(128)(4,1)} %bitcast.140), calls=%async_computation.2 | async-start | bytes 8388608
  106.0 36.9 %copy-start.7 = (bf16[48,8,8,128]{3,2,1,0:T(8,128)(2,1)}, bf16[48,8,8,128]{3,2,1,0:T(8,128)(2,1)S(1)}, u32[]{:S(2)}) copy-start(bf16[48,8,8,128]{3,2,1,0:T(8,128)(2,1)S(1)} %copy.171) | copy-start | bytes 2359300
  106.0 35.9 %slice-start.2 = ((s8[6291456]{0:T(1024)(128)(4,1)}), s8[4194304]{0:T(1024)(128)(4,1)S(1)}, s32[]{:S(2)}) async-start(s8[6291456]{0:T(1024)(128)(4,1)} %bitcast.149), calls=%async_computation.3 | async-start | bytes 8388608
  110.4 2.0 copy-start.9
  110.4 31.5 %slice-start.3 = ((s8[6291456]{0:T(1024)(128)(4,1)}), s8[2097152]{0:T(1024)(128)(4,1)S(1)}, s32[]{:S(2)}) async-start(s8[6291456]{0:T(1024)(128)(4,1)} %bitcast.149), calls=%async_computation.4 | async-start | bytes 4194304
  112.4 30.5 %copy-start.14 = (f32[384,8,128]{0,2,1:T(8,128)}, f32[384,8,128]{0,2,1:T(8,128)S(1)}, u32[]{:S(2)}) copy-start(f32[384,8,128]{0,2,1:T(8,128)S(1)} %fusion.30) | copy-start | bytes 4718596
  116.0 26.9 %copy-start.4 = (bf16[512,1024]{0,1:T(8,128)(2,1)S(1)}, bf16[512,1024]{0,1:T(8,128)(2,1)}, u32[]{:S(2)}) copy-start(bf16[512,1024]{0,1:T(8,128)(2,1)} %copy.139) | copy-start | bytes 3145732
  116.0 30.9 %collective-permute-start.2 = (f32[8,128]{1,0:T(8,128)S(1)}, f32[8,128]{1,0:T(8,128)S(1)}, u32[]{:S(2)}, u32[]{:S(2)}) collective-permute-start(f32[8,128]{1,0:T(8,128)S(1)} %get-tuple-element.54), channel_id=1, source_target_pairs={{4,0},{8,4},{12,8},{16,12},{20,16},{24,20},{28,24},{32,28},{36,32}... | collective-permute-start | bytes 12296 | tf_op jit(solution)/shard_map/ppermute | solution.py:29
  125.3 23.6 %collective-permute-start.4 = (f32[8,128]{1,0:T(8,128)S(1)}, f32[8,128]{1,0:T(8,128)S(1)}, u32[]{:S(2)}, u32[]{:S(2)}) collective-permute-start(f32[8,128]{1,0:T(8,128)S(1)} %get-tuple-element.55), channel_id=1, source_target_pairs={{0,4},{4,8},{8,12},{12,16},{16,20},{20,24},{24,28},{28,32},{32,36}... | collective-permute-start | bytes 12296 | tf_op jit(solution)/shard_map/ppermute | solution.py:29
  127.2 21.7 %collective-permute-start.3 = (f32[8,128]{1,0:T(8,128)S(1)}, f32[8,128]{1,0:T(8,128)S(1)}, u32[]{:S(2)}, u32[]{:S(2)}) collective-permute-start(f32[8,128]{1,0:T(8,128)S(1)} %get-tuple-element.52), channel_id=1, source_target_pairs={{4,0},{8,4},{12,8},{16,12},{20,16},{24,20},{28,24},{32,28},{36,32}... | collective-permute-start | bytes 12296 | tf_op jit(solution)/shard_map/ppermute | solution.py:29
  132.9 15.9 %collective-permute-start.5 = (f32[8,128]{1,0:T(8,128)S(1)}, f32[8,128]{1,0:T(8,128)S(1)}, u32[]{:S(2)}, u32[]{:S(2)}) collective-permute-start(f32[8,128]{1,0:T(8,128)S(1)} %get-tuple-element.53), channel_id=1, source_target_pairs={{0,4},{4,8},{8,12},{12,16},{16,20},{20,24},{24,28},{28,32},{32,36}... | collective-permute-start | bytes 12296 | tf_op jit(solution)/shard_map/ppermute | solution.py:29
  135.9 48.0 %collective-permute-start.6 = (f32[128,8,128]{0,2,1:T(8,128)}, f32[128,8,128]{0,2,1:T(8,128)}, u32[]{:S(2)}, u32[]{:S(2)}) collective-permute-start(f32[128,8,128]{0,2,1:T(8,128)} %get-tuple-element.43), channel_id=1, source_target_pairs={{4,0},{8,4},{12,8},{16,12},{20,16},{24,20},{28,24},{32,28},{36,32}... | collective-permute-start | bytes 1572872 | tf_op jit(solution)/shard_map/ppermute | solution.py:29
  143.7 31.6 %copy-start.10 = (bf16[384,8,128]{0,2,1:T(8,128)(2,1)S(1)}, bf16[384,8,128]{0,2,1:T(8,128)(2,1)}, u32[]{:S(2)}) copy-start(bf16[384,8,128]{0,2,1:T(8,128)(2,1)} %copy.149) | copy-start | bytes 2359300
  146.9 37.1 %collective-permute-start.7 = (f32[128,8,128]{0,2,1:T(8,128)}, f32[128,8,128]{0,2,1:T(8,128)}, u32[]{:S(2)}, u32[]{:S(2)}) collective-permute-start(f32[128,8,128]{0,2,1:T(8,128)} %get-tuple-element.44), channel_id=1, source_target_pairs={{0,4},{4,8},{8,12},{12,16},{16,20},{20,24},{24,28},{28,32},{32,36}... | collective-permute-start | bytes 1572872 | tf_op jit(solution)/shard_map/ppermute | solution.py:29
  148.9 16.7 %collective-permute-start.11 = (f32[8,128]{1,0:T(8,128)S(1)}, f32[8,128]{1,0:T(8,128)S(1)}, u32[]{:S(2)}, u32[]{:S(2)}) collective-permute-start(f32[8,128]{1,0:T(8,128)S(1)} %get-tuple-element.50), channel_id=1, source_target_pairs={{4,0},{8,4},{12,8},{16,12},{20,16},{24,20},{28,24},{32,28},{36,32}... | collective-permute-start | bytes 12296 | tf_op jit(solution)/shard_map/ppermute | solution.py:21
  154.7 12.9 %collective-permute-start.10 = (f32[8,128]{1,0:T(8,128)S(1)}, f32[8,128]{1,0:T(8,128)S(1)}, u32[]{:S(2)}, u32[]{:S(2)}) collective-permute-start(f32[8,128]{1,0:T(8,128)S(1)} %get-tuple-element.50), channel_id=1, source_target_pairs={{0,4},{4,8},{8,12},{12,16},{16,20},{20,24},{24,28},{28,32},{32,36}... | collective-permute-start | bytes 12296 | tf_op jit(solution)/shard_map/ppermute | solution.py:20
  159.9 33.4 %collective-permute-start.16 = (bf16[128,8,128]{0,2,1:T(8,128)(2,1)}, bf16[128,8,128]{0,2,1:T(8,128)(2,1)}, u32[]{:S(2)}, u32[]{:S(2)}) collective-permute-start(bf16[128,8,128]{0,2,1:T(8,128)(2,1)} %get-tuple-element.45), channel_id=1, source_target_pairs={{4,0},{8,4},{12,8},{16,12},{20,16},{24,20},{28,24},{32,28},{36,32}... | collective-permute-start | bytes 786440 | tf_op jit(solution)/shard_map/ppermute | solution.py:29
  165.6 7.7 %collective-permute-start.8 = (f32[8,128]{1,0:T(8,128)S(1)}, f32[8,128]{1,0:T(8,128)S(1)}, u32[]{:S(2)}, u32[]{:S(2)}) collective-permute-start(f32[8,128]{1,0:T(8,128)S(1)} %get-tuple-element.39), channel_id=1, source_target_pairs={{0,4},{4,8},{8,12},{12,16},{16,20},{20,24},{24,28},{28,32},{32,36}... | collective-permute-start | bytes 12296 | tf_op jit(solution)/shard_map/ppermute | solution.py:20
  167.6 7.7 %collective-permute-start.9 = (f32[8,128]{1,0:T(8,128)S(1)}, f32[8,128]{1,0:T(8,128)S(1)}, u32[]{:S(2)}, u32[]{:S(2)}) collective-permute-start(f32[8,128]{1,0:T(8,128)S(1)} %get-tuple-element.39), channel_id=1, source_target_pairs={{4,0},{8,4},{12,8},{16,12},{20,16},{24,20},{28,24},{32,28},{36,32}... | collective-permute-start | bytes 12296 | tf_op jit(solution)/shard_map/ppermute | solution.py:21
  173.3 19.9 %collective-permute-start.17 = (bf16[128,8,128]{0,2,1:T(8,128)(2,1)}, bf16[128,8,128]{0,2,1:T(8,128)(2,1)}, u32[]{:S(2)}, u32[]{:S(2)}) collective-permute-start(bf16[128,8,128]{0,2,1:T(8,128)(2,1)} %get-tuple-element.46), channel_id=1, source_target_pairs={{0,4},{4,8},{8,12},{12,16},{16,20},{20,24},{24,28},{28,32},{32,36}... | collective-permute-start | bytes 786440 | tf_op jit(solution)/shard_map/ppermute | solution.py:29
  175.3 8.7 %copy-start.11 = (f32[1,128,1024]{1,2,0:T(8,128)S(1)}, f32[1,128,1024]{1,2,0:T(8,128)}, u32[]{:S(2)}) copy-start(f32[1,128,1024]{1,2,0:T(8,128)} %copy.146) | copy-start | bytes 1572868
  181.6 16.7 %copy-start.8 = (bf16[48,8,8,128]{3,2,1,0:T(8,128)(2,1)S(1)}, bf16[48,8,8,128]{3,2,1,0:T(8,128)(2,1)}, u32[]{:S(2)}) copy-start(bf16[48,8,8,128]{3,2,1,0:T(8,128)(2,1)} %copy-done.7) | copy-start | bytes 2359300
  181.6 16.7 %copy-start.13 = (pred[48,8,4,128]{3,1,2,0:T(8,128)(4,1)S(1)}, pred[48,8,4,128]{3,1,2,0:T(8,128)(4,1)}, u32[]{:S(2)}) copy-start(pred[48,8,4,128]{3,1,2,0:T(8,128)(4,1)} %copy.190) | copy-start | bytes 589828
  185.6 10.7 %collective-permute-start.13 = (f32[8,128]{1,0:T(8,128)S(1)}, f32[8,128]{1,0:T(8,128)S(1)}, u32[]{:S(2)}, u32[]{:S(2)}) collective-permute-start(f32[8,128]{1,0:T(8,128)S(1)} %bitcast.181), channel_id=1, source_target_pairs={{4,0},{8,4},{12,8},{16,12},{20,16},{24,20},{28,24},{32,28},{36,32}... | collective-permute-start | bytes 12296 | tf_op jit(solution)/shard_map/ppermute | solution.py:21
  191.3 7.0 %collective-permute-start.12 = (f32[8,128]{1,0:T(8,128)S(1)}, f32[8,128]{1,0:T(8,128)S(1)}, u32[]{:S(2)}, u32[]{:S(2)}) collective-permute-start(f32[8,128]{1,0:T(8,128)S(1)} %bitcast.182), channel_id=1, source_target_pairs={{0,4},{4,8},{8,12},{12,16},{16,20},{20,24},{24,28},{28,32},{32,36}... | collective-permute-start | bytes 12296 | tf_op jit(solution)/shard_map/ppermute | solution.py:20
  198.4 8.3 %copy-start.3 = (bf16[512,1024]{0,1:T(8,128)(2,1)S(1)}, bf16[512,1024]{0,1:T(8,128)(2,1)}, u32[]{:S(2)}) copy-start(bf16[512,1024]{0,1:T(8,128)(2,1)} %copy.169) | copy-start | bytes 3145732
  206.6 8.0 %copy-start.6 = (bf16[384,8,128]{0,2,1:T(8,128)(2,1)S(1)}, bf16[384,8,128]{0,2,1:T(8,128)(2,1)}, u32[]{:S(2)}) copy-start(bf16[384,8,128]{0,2,1:T(8,128)(2,1)} %copy-done.5) | copy-start | bytes 2359300
  206.7 17.8 %copy-start.1 = (bf16[512,1024]{1,0:T(8,128)(2,1)S(1)}, bf16[512,1024]{1,0:T(8,128)(2,1)}, u32[]{:S(2)}) copy-start(bf16[512,1024]{1,0:T(8,128)(2,1)} %param.9) | copy-start | bytes 3145732
  209.0 7.7 %collective-permute-start.14 = (bf16[128,8,128]{0,2,1:T(8,128)(2,1)S(1)}, bf16[128,8,128]{0,2,1:T(8,128)(2,1)S(1)}, u32[]{:S(2)}, u32[]{:S(2)}) collective-permute-start(bf16[128,8,128]{0,2,1:T(8,128)(2,1)S(1)} %get-tuple-element.47), channel_id=1, source_target_pairs={{4,0},{8,4},{12,8},{16,12},{20,16},{24,20},{28,24},{32,28},{36,32}... | collective-permute-start | bytes 786440 | tf_op jit(solution)/shard_map/ppermute | solution.py:29
  212.7 9.8 %collective-permute-start.15 = (bf16[128,8,128]{0,2,1:T(8,128)(2,1)S(1)}, bf16[128,8,128]{0,2,1:T(8,128)(2,1)S(1)}, u32[]{:S(2)}, u32[]{:S(2)}) collective-permute-start(bf16[128,8,128]{0,2,1:T(8,128)(2,1)S(1)} %get-tuple-element.48), channel_id=1, source_target_pairs={{0,4},{4,8},{8,12},{12,16},{16,20},{20,24},{24,28},{28,32},{32,36}... | collective-permute-start | bytes 786440 | tf_op jit(solution)/shard_map/ppermute | solution.py:29
where the time goes:
time: 226 us; the launch traced here: 224 us
  starting transfers between devices  77.2 us (34%)
  waiting for transfers between devices  59 us (26%)
  matrix products  37.3 us (17%)
  local copies, waits for them, and re-layouts  36.6 us (16%)
  other arithmetic  13 us (6%)
    ppermute x10, starting transfers between devices, from_behind(): return lax.ppermute(block, axis, route)  39.9 us
    all_to_all x1, waiting for transfers between devices, on_device(): lax.all_to_all(window, 'text', split_axis=2, concat_axis=1, tiled=True)  37.6 us
    ppermute x4, starting transfers between devices, extended(): after = lax.ppermute(initial, axis, down)  24.6 us
    unnamed x57, local copies, waits for them, and re-layouts  12.1 us
    dot_general x1, matrix products, on_device(): jnp.einsum('fhd,thd->hft', frame_g, values_win, preferred_element_type=jn...  8.24 us
    ppermute x4, waiting for transfers between devices, extended(): before = lax.ppermute(last, axis, up)  8.03 us
    ppermute x4, starting transfers between devices, extended(): before = lax.ppermute(last, axis, up)  7.68 us
    ppermute x4, waiting for transfers between devices, extended(): after = lax.ppermute(initial, axis, down)  7.57 us
  transfers between devices with their start and end apart: 19, of which 5 were waited for; matrix products, arithmetic and copies ran while one was open for 13% of the time, Pallas kernels for 0%

commit v1 on v0

--- a/solution.py
+++ b/solution.py
@@ -4,6 +4,7 @@
 import jax.numpy as jnp
 from jax import lax
 from jax.sharding import PartitionSpec as P
+from jax.lax import all_to_all, axis_size
 
 HEAD_DIM = 128
 BLOCK = 128
@@ -48,12 +49,18 @@
     band_first,
     band_count,
 ):
+
+    def apply_squares_in(obj):
+        return jnp.concatenate(
+            all_to_all(jnp.stack(jnp.split(obj, axis_size("text"), axis=2)), "text", 0, 0), axis=1
+        )
+
     score_scale = 1.0 / math.sqrt(HEAD_DIM)
     stacked = jnp.stack([text_keys, text_values, text_grads])
     group_count = lax.axis_size("text")
     rows_sub = stacked.shape[1]
     window = extended(stacked, (("frame", 1),), rows_sub)
-    arrived = lax.all_to_all(window, "text", split_axis=2, concat_axis=1, tiled=True)
+    arrived = apply_squares_in(window)
     head_width = arrived.shape[2]
     arrived = arrived.reshape(3, group_count, 3, rows_sub, head_width).transpose(0, 2, 1, 3, 4)
     own_rows = group_count * rows_sub

time: 226 us -> 189 us (0.84)
  waiting for transfers between devices: 59 us -> 39.7 us
  local copies, waits for them, and re-layouts: 36.6 us -> 25.7 us
  starting transfers between devices: 77.2 us -> 70.4 us
    all_to_all x1, waiting for transfers between devices: 37.6 us -> 22.1 us  [apply_squares_in(): all_to_all(jnp.stack(jnp.split(obj, axis_size('text'), axis=2)), 'text',...]
    ppermute x10, starting transfers between devices: 39.9 us -> 33.7 us  [from_behind(): return lax.ppermute(block, axis, route)]
    ppermute x4, waiting for transfers between devices: 7.57 us -> 1.76 us  [extended(): after = lax.ppermute(initial, axis, down)]
    all_to_all x1, local copies, waits for them, and re-layouts: 5.47 us -> 0.28 us  [apply_squares_in(): all_to_all(jnp.stack(jnp.split(obj, axis_size('text'), axis=2)), 'text',...]
    concatenate x1 -> x0, local copies, waits for them, and re-layouts: 4.75 us -> none  [extended(): array = jnp.concatenate([before, array, after], axis=dim)]
    dot_general x1, matrix products: 5.5 us -> 3.04 us  [on_device(): jnp.einsum('fhd,thd->hft', frame_k, keys_win, preferred_element_type=jnp....]
    reduce_sum x1, other arithmetic: 4.32 us -> 2.02 us  [on_device(): col_total = jnp.sum(col_exp, axis=1)]
    ppermute x10, waiting for transfers between devices: 5.85 us -> 8.11 us  [from_behind(): return lax.ppermute(block, axis, route)]
  transfers between devices with their start and end apart: 19 -> 19, of which waited for: 5 -> 5; matrix products, arithmetic and copies ran while one was open for 13% -> 20% of each run, Pallas kernels for 0% -> 0%
where the time goes in v1:
time: 189 us; the launch traced here: 188 us
  starting transfers between devices  70.4 us (37%)
  waiting for transfers between devices  39.7 us (21%)
  matrix products  38.4 us (20%)
  local copies, waits for them, and re-layouts  25.7 us (14%)
  other arithmetic  12.4 us (7%)
    ppermute x10, starting transfers between devices, from_behind(): return lax.ppermute(block, axis, route)  33.7 us
    ppermute x4, starting transfers between devices, extended(): after = lax.ppermute(initial, axis, down)  24.6 us
    all_to_all x1, waiting for transfers between devices, apply_squares_in(): all_to_all(jnp.stack(jnp.split(obj, axis_size('text'), axis=2)), 'text',...  22.1 us
    unnamed x47, local copies, waits for them, and re-layouts  13.2 us
    dot_general x1, matrix products, on_device(): jnp.einsum('fhd,thd->hft', frame_g, values_win, preferred_element_type=jn...  8.24 us
    ppermute x10, waiting for transfers between devices, from_behind(): return lax.ppermute(block, axis, route)  8.11 us
    sub x1, matrix products, on_device(): scores - row_max[:, :, None]  7.92 us
    ppermute x4, waiting for transfers between devices, extended(): before = lax.ppermute(last, axis, up)  7.74 us
  transfers between devices with their start and end apart: 19, of which 5 were waited for; matrix products, arithmetic and copies ran while one was open for 20% of the time, Pallas kernels for 0%

profile of v1, /device:TPU:24, one launch (start us, length us, event | category | flops | bytes accessed | tf_op | source)
XLA Modules:
  0.0 187.8 jit_solution(5245905996809524340)
XLA Ops:
  0.6 1.3 pad_maximum_fusion.2
  1.9 1.9 %collective-permute-start = (bf16[3,32,4096]{2,1,0:T(8,128)(2,1)S(1)}, bf16[3,32,4096]{2,1,0:T(8,128)(2,1)S(1)}, u32[]{:S(2)}, u32[]{:S(2)}) collective-permute-start(bf16[3,32,4096]{2,1,0:T(8,128)(2,1)S(1)} %pad_maximum_fusion.2), channel_id=1, source_target_pairs={{0,4},{4,8},{8,12},{12,16},{16,20},{20,24},{24,28},{28,32},{32,36}... | collective-permute-start | bytes 2359304 | tf_op jit(solution)/shard_map/ppermute | solution.py:21
  3.9 7.4 %collective-permute-start.1 = (bf16[3,32,4096]{2,1,0:T(8,128)(2,1)S(1)}, bf16[3,32,4096]{2,1,0:T(8,128)(2,1)S(1)}, u32[]{:S(2)}, u32[]{:S(2)}) collective-permute-start(bf16[3,32,4096]{2,1,0:T(8,128)(2,1)S(1)} %pad_maximum_fusion.2), channel_id=1, source_target_pairs={{4,0},{8,4},{12,8},{16,12},{20,16},{24,20},{28,24},{32,28},{36,32}... | collective-permute-start | bytes 2359304 | tf_op jit(solution)/shard_map/ppermute | solution.py:22
  11.3 7.7 %collective-permute-done = bf16[3,32,4096]{2,1,0:T(8,128)(2,1)S(1)} collective-permute-done((bf16[3,32,4096]{2,1,0:T(8,128)(2,1)S(1)}, bf16[3,32,4096]{2,1,0:T(8,128)(2,1)S(1)}, u32[]{:S(2)}, u32[]{:S(2)}) %collective-permute-start) | collective-permute-done | bytes 786464 | tf_op jit(solution)/shard_map/ppermute | solution.py:21
  19.0 1.8 collective-permute-done.1
  20.7 1.3 pad_maximum_fusion
  22.3 1.7 pad_maximum_fusion.1
  24.0 4.3 %all-to-all-start = ((bf16[4,3,96,1024]{3,2,1,0:T(8,128)(2,1)}), bf16[4,3,96,1024]{3,2,1,0:T(8,128)(2,1)S(1)}, u32[]{:S(2)}, u32[]{:S(2)}) async-start(bf16[4,3,96,1024]{3,2,1,0:T(8,128)(2,1)} %pad_maximum_fusion.1), calls=%async_computation | async-start | bytes 4718592 | tf_op jit(solution)/shard_map/all_to_all | solution.py:55
  29.4 2.3 %copy.131 = bf16[512,1024]{0,1:T(8,128)(2,1)} copy(bf16[512,1024]{1,0:T(8,128)(2,1)} %param.8) | data formatting | bytes 2097152 | tf_op jit(solution)/shard_map/reshape | solution.py:76
  31.7 2.3 %copy.102 = bf16[512,1024]{0,1:T(8,128)(2,1)} copy(bf16[512,1024]{1,0:T(8,128)(2,1)} %param.10) | data formatting | bytes 2097152 | tf_op args[2]
  34.0 22.1 %all-to-all-done = bf16[4,3,96,1024]{3,2,1,0:T(8,128)(2,1)S(1)} async-done(((bf16[4,3,96,1024]{3,2,1,0:T(8,128)(2,1)}), bf16[4,3,96,1024]{3,2,1,0:T(8,128)(2,1)S(1)}, u32[]{:S(2)}, u32[]{:S(2)}) %all-to-all-start) | async-done | bytes 2359328 | tf_op jit(solution)/shard_map/all_to_all | solution.py:55
  56.4 1.4 fusion.61
  58.9 2.4 %copy.110 = bf16[384,8,128]{0,2,1:T(8,128)(2,1)} copy(bf16[384,8,128]{2,1,0:T(8,128)(2,1)} %bitcast.157) | data formatting | bytes 1572864 | tf_op jit(solution)/shard_map/reshape;squeeze | solution.py:72
  61.3 7.9 %fusion.67 = (f32[8,512]{1,0:T(8,128)S(1)}, f32[8,512,384]{1,2,0:T(8,128)}) fusion(pred[512,384]{0,1:T(8,128)(4,1)} %bitcast.165, bf16[384,8,128]{0,2,1:T(8,128)(2,1)} %copy.110, bf16[512,8,128]{0,2,1:T(8,128)(2,1)} %bitcast.148), kind=kOutput, calls=%fused_computation.97 | convolution fusion | flops 814743936 | bytes 8339456 | tf_op jit(solution)/shard_map/sub | solution.py:87
  69.2 3.0 %fusion.10 = (f32[8,384]{1,0:T(8,128)S(1)}, f32[8,384,512]{2,1,0:T(8,128)S(1)}) fusion(pred[512,384]{0,1:T(8,128)(4,1)} %bitcast.166, bf16[384,8,128]{0,2,1:T(8,128)(2,1)} %copy.110, bf16[512,8,128]{0,2,1:T(8,128)(2,1)} %bitcast.149), kind=kOutput, calls=%fused_computation.16 | convolution fusion | flops 407368704 | bytes 8335360 | tf_op jit(solution)/shard_map/fhd,thd->hft/dot_general | solution.py:83
  74.3 2.2 %fusion.69 = (bf16[384,8,128]{0,2,1:T(8,128)(2,1)S(1)}, f32[384,8,128]{0,2,1:T(8,128)}) fusion(bf16[8,512,384]{1,2,0:T(8,128)(2,1)S(1)} %fusion.26, bf16[512,8,128]{0,2,1:T(8,128)(2,1)S(1)} %bitcast.152), kind=kOutput, calls=%fused_computation.99 | convolution fusion | flops 403046400 | bytes 6553600 | tf_op jit(solution)/shard_map/hft,fhd->thd/dot_general | solution.py:152
  77.5 6.4 %collective-permute-start.16 = (bf16[128,8,128]{0,2,1:T(8,128)(2,1)}, bf16[128,8,128]{0,2,1:T(8,128)(2,1)}, u32[]{:S(2)}, u32[]{:S(2)}) collective-permute-start(bf16[128,8,128]{0,2,1:T(8,128)(2,1)} %get-tuple-element.43), channel_id=1, source_target_pairs={{4,0},{8,4},{12,8},{16,12},{20,16},{24,20},{28,24},{32,28},{36,32}... | collective-permute-start | bytes 786440 | tf_op jit(solution)/shard_map/ppermute | solution.py:30
  83.9 2.0 %fusion.12 = f32[8,384]{1,0:T(8,128)S(1)} fusion(f32[8,384,512]{2,1,0:T(8,128)S(1)} %get-tuple-element.57, f32[8,384]{1,0:T(8,128)S(1)} %get-tuple-element.56, pred[512,384]{0,1:T(8,128)(4,1)S(1)} %bitcast.168), kind=kLoop, calls=%fused_computation.18 | loop fusion | flops 6288384 | bytes 6512640 | tf_op jit(solution)/shard_map/reduce_sum | solution.py:97
  86.0 1.9 %collective-permute-start.2 = (f32[8,128]{1,0:T(8,128)S(1)}, f32[8,128]{1,0:T(8,128)S(1)}, u32[]{:S(2)}, u32[]{:S(2)}) collective-permute-start(f32[8,128]{1,0:T(8,128)S(1)} %get-tuple-element.52), channel_id=1, source_target_pairs={{4,0},{8,4},{12,8},{16,12},{20,16},{24,20},{28,24},{32,28},{36,32}... | collective-permute-start | bytes 12296 | tf_op jit(solution)/shard_map/ppermute | solution.py:30
  87.9 2.4 %collective-permute-start.4 = (f32[8,128]{1,0:T(8,128)S(1)}, f32[8,128]{1,0:T(8,128)S(1)}, u32[]{:S(2)}, u32[]{:S(2)}) collective-permute-start(f32[8,128]{1,0:T(8,128)S(1)} %get-tuple-element.53), channel_id=1, source_target_pairs={{0,4},{4,8},{8,12},{12,16},{16,20},{20,24},{24,28},{28,32},{32,36}... | collective-permute-start | bytes 12296 | tf_op jit(solution)/shard_map/ppermute | solution.py:30
  90.3 5.3 %collective-permute-start.3 = (f32[8,128]{1,0:T(8,128)S(1)}, f32[8,128]{1,0:T(8,128)S(1)}, u32[]{:S(2)}, u32[]{:S(2)}) collective-permute-start(f32[8,128]{1,0:T(8,128)S(1)} %get-tuple-element.50), channel_id=1, source_target_pairs={{4,0},{8,4},{12,8},{16,12},{20,16},{24,20},{28,24},{32,28},{36,32}... | collective-permute-start | bytes 12296 | tf_op jit(solution)/shard_map/ppermute | solution.py:30
  95.6 2.2 %collective-permute-start.5 = (f32[8,128]{1,0:T(8,128)S(1)}, f32[8,128]{1,0:T(8,128)S(1)}, u32[]{:S(2)}, u32[]{:S(2)}) collective-permute-start(f32[8,128]{1,0:T(8,128)S(1)} %get-tuple-element.51), channel_id=1, source_target_pairs={{0,4},{4,8},{8,12},{12,16},{16,20},{20,24},{24,28},{28,32},{32,36}... | collective-permute-start | bytes 12296 | tf_op jit(solution)/shard_map/ppermute | solution.py:30
  97.9 2.1 %fusion.30 = f32[384,8,128]{0,2,1:T(8,128)S(1)} fusion(f32[8,384,512]{2,1,0:T(8,128)S(1)} %get-tuple-element.57, f32[8,384]{1,0:T(8,128)S(1)} %get-tuple-element.56, pred[512,384]{0,1:T(8,128)(4,1)S(1)} %bitcast.169, bf16[512,1024]{1,0:T(8,128)(2,1)S(1)} %copy-done), kind=kOutput, calls=%fused_computation.41 | convolution fusion | flops 408944640 | bytes 9121792 | tf_op jit(solution)/shard_map/hft,fhd->thd/dot_general | solution.py:99
  100.0 1.3 fusion.62
  101.3 1.7 copy.108
  104.3 1.4 copy.112
  105.7 4.8 %fusion.34 = f32[8,384,512]{2,1,0:T(8,128)} fusion(bf16[384,8,128]{0,2,1:T(8,128)(2,1)} %copy.112, bf16[512,1024]{1,0:T(8,128)(2,1)S(1)} %copy-done), kind=kOutput, calls=%fused_computation.43 | convolution fusion | flops 402653184 | bytes 8126464 | tf_op jit(solution)/shard_map/fhd,thd->hft/dot_general | solution.py:134
  111.7 1.3 copy.117
  113.0 1.9 %collective-permute-start.17 = (bf16[128,8,128]{0,2,1:T(8,128)(2,1)}, bf16[128,8,128]{0,2,1:T(8,128)(2,1)}, u32[]{:S(2)}, u32[]{:S(2)}) collective-permute-start(bf16[128,8,128]{0,2,1:T(8,128)(2,1)} %get-tuple-element.44), channel_id=1, source_target_pairs={{0,4},{4,8},{8,12},{12,16},{16,20},{20,24},{24,28},{28,32},{32,36}... | collective-permute-start | bytes 786440 | tf_op jit(solution)/shard_map/ppermute | solution.py:30
  114.9 5.8 %collective-permute-start.6 = (f32[128,8,128]{0,2,1:T(8,128)}, f32[128,8,128]{0,2,1:T(8,128)}, u32[]{:S(2)}, u32[]{:S(2)}) collective-permute-start(f32[128,8,128]{0,2,1:T(8,128)} %get-tuple-element.41), channel_id=1, source_target_pairs={{4,0},{8,4},{12,8},{16,12},{20,16},{24,20},{28,24},{32,28},{36,32}... | collective-permute-start | bytes 1572872 | tf_op jit(solution)/shard_map/ppermute | solution.py:30
  120.7 1.9 %collective-permute-start.8 = (f32[8,128]{1,0:T(8,128)S(1)}, f32[8,128]{1,0:T(8,128)S(1)}, u32[]{:S(2)}, u32[]{:S(2)}) collective-permute-start(f32[8,128]{1,0:T(8,128)S(1)} %get-tuple-element.33), channel_id=1, source_target_pairs={{0,4},{4,8},{8,12},{12,16},{16,20},{20,24},{24,28},{28,32},{32,36}... | collective-permute-start | bytes 12296 | tf_op jit(solution)/shard_map/ppermute | solution.py:21
  122.7 5.8 %collective-permute-start.9 = (f32[8,128]{1,0:T(8,128)S(1)}, f32[8,128]{1,0:T(8,128)S(1)}, u32[]{:S(2)}, u32[]{:S(2)}) collective-permute-start(f32[8,128]{1,0:T(8,128)S(1)} %get-tuple-element.33), channel_id=1, source_target_pairs={{4,0},{8,4},{12,8},{16,12},{20,16},{24,20},{28,24},{32,28},{36,32}... | collective-permute-start | bytes 12296 | tf_op jit(solution)/shard_map/ppermute | solution.py:22
  128.4 1.9 %collective-permute-start.10 = (f32[8,128]{1,0:T(8,128)S(1)}, f32[8,128]{1,0:T(8,128)S(1)}, u32[]{:S(2)}, u32[]{:S(2)}) collective-permute-start(f32[8,128]{1,0:T(8,128)S(1)} %get-tuple-element.48), channel_id=1, source_target_pairs={{0,4},{4,8},{8,12},{12,16},{16,20},{20,24},{24,28},{28,32},{32,36}... | collective-permute-start | bytes 12296 | tf_op jit(solution)/shard_map/ppermute | solution.py:21
  130.4 5.8 %collective-permute-start.11 = (f32[8,128]{1,0:T(8,128)S(1)}, f32[8,128]{1,0:T(8,128)S(1)}, u32[]{:S(2)}, u32[]{:S(2)}) collective-permute-start(f32[8,128]{1,0:T(8,128)S(1)} %get-tuple-element.48), channel_id=1, source_target_pairs={{4,0},{8,4},{12,8},{16,12},{20,16},{24,20},{28,24},{32,28},{36,32}... | collective-permute-start | bytes 12296 | tf_op jit(solution)/shard_map/ppermute | solution.py:22
  136.2 1.9 %collective-permute-start.7 = (f32[128,8,128]{0,2,1:T(8,128)}, f32[128,8,128]{0,2,1:T(8,128)}, u32[]{:S(2)}, u32[]{:S(2)}) collective-permute-start(f32[128,8,128]{0,2,1:T(8,128)} %get-tuple-element.42), channel_id=1, source_target_pairs={{0,4},{4,8},{8,12},{12,16},{16,20},{20,24},{24,28},{28,32},{32,36}... | collective-permute-start | bytes 1572872 | tf_op jit(solution)/shard_map/ppermute | solution.py:30
  138.1 6.3 %fusion.27 = bf16[8,128,512]{2,1,0:T(8,128)(2,1)} fusion(bf16[384,8,128]{0,2,1:T(8,128)(2,1)S(1)} %copy-done.12, f32[8,384,512]{2,1,0:T(8,128)} %copy-done.2, f32[8,384]{1,0:T(8,128)S(1)} %compare_select_fusion, f32[8,384]{1,0:T(8,128)S(1)} %pad_maximum_fusion.3, pred[512,384]{0,1:T(8,128)(4,1)} %bitcast.167), kind=kOutput, calls=%fused_computation.38 | convolution fusion | flops 411041792 | bytes 8347648 | tf_op jit(solution)/shard_map/hft,thd->fhd/dot_general | solution.py:143
  144.4 2.4 %copy.120 = bf16[512,1024]{1,0:T(8,128)(2,1)} copy(bf16[512,1024]{0,1:T(8,128)(2,1)} %bitcast.174) | data formatting | bytes 2097152
  146.8 2.3 %collective-permute-done.7 = f32[128,8,128]{0,2,1:T(8,128)} collective-permute-done((f32[128,8,128]{0,2,1:T(8,128)}, f32[128,8,128]{0,2,1:T(8,128)}, u32[]{:S(2)}, u32[]{:S(2)}) %collective-permute-start.7) | collective-permute-done | bytes 524320 | tf_op jit(solution)/shard_map/ppermute | solution.py:30
  149.1 1.6 multiply_reduce_fusion.1
  150.7 1.9 %collective-permute-start.12 = (f32[8,128]{1,0:T(8,128)S(1)}, f32[8,128]{1,0:T(8,128)S(1)}, u32[]{:S(2)}, u32[]{:S(2)}) collective-permute-start(f32[8,128]{1,0:T(8,128)S(1)} %bitcast.184), channel_id=1, source_target_pairs={{0,4},{4,8},{8,12},{12,16},{16,20},{20,24},{24,28},{28,32},{32,36}... | collective-permute-start | bytes 12296 | tf_op jit(solution)/shard_map/ppermute | solution.py:21
  152.6 5.8 %collective-permute-start.13 = (f32[8,128]{1,0:T(8,128)S(1)}, f32[8,128]{1,0:T(8,128)S(1)}, u32[]{:S(2)}, u32[]{:S(2)}) collective-permute-start(f32[8,128]{1,0:T(8,128)S(1)} %bitcast.185), channel_id=1, source_target_pairs={{4,0},{8,4},{12,8},{16,12},{20,16},{24,20},{28,24},{32,28},{36,32}... | collective-permute-start | bytes 12296 | tf_op jit(solution)/shard_map/ppermute | solution.py:22
  158.4 1.3 fusion.42
  161.4 8.2 %fusion.2 = bf16[8,512,384]{1,2,0:T(8,128)(2,1)S(1)} fusion(f32[8,384,512]{2,1,0:T(8,128)} %fusion.34, f32[8,384]{1,0:T(8,128)S(1)} %pad_maximum_fusion.4, f32[8,512]{1,0:T(8,128)S(1)} %bitcast.183, bf16[512,8,128]{0,2,1:T(8,128)(2,1)S(1)} %bitcast.153, f32[8,512,384]{1,2,0:T(8,128)} %get-tuple-element.55, f32[8,512]{1,0:T(8,128)S(1)} %get-tuple-element.54, ...), kind=kOutput, calls=%fused_computation.3 | convolution fusion | flops 419954688 | bytes 24121344 | tf_op jit(solution)/shard_map/fhd,thd->hft/dot_general | solution.py:133
  169.7 2.2 %fusion.68 = (bf16[384,8,128]{0,2,1:T(8,128)(2,1)S(1)}, f32[384,8,128]{0,2,1:T(8,128)}) fusion(bf16[8,512,384]{1,2,0:T(8,128)(2,1)S(1)} %fusion.2, bf16[512,8,128]{0,2,1:T(8,128)(2,1)S(1)} %bitcast.150), kind=kOutput, calls=%fused_computation.98 | convolution fusion | flops 403439616 | bytes 6553600 | tf_op jit(solution)/shard_map/hft,fhd->thd/dot_general | solution.py:149
  172.0 4.0 %collective-permute-start.14 = (bf16[128,8,128]{0,2,1:T(8,128)(2,1)S(1)}, bf16[128,8,128]{0,2,1:T(8,128)(2,1)S(1)}, u32[]{:S(2)}, u32[]{:S(2)}) collective-permute-start(bf16[128,8,128]{0,2,1:T(8,128)(2,1)S(1)} %get-tuple-element.45), channel_id=1, source_target_pairs={{4,0},{8,4},{12,8},{16,12},{20,16},{24,20},{28,24},{32,28},{36,32}... | collective-permute-start | bytes 786440 | tf_op jit(solution)/shard_map/ppermute | solution.py:30
  176.0 1.9 %collective-permute-start.15 = (bf16[128,8,128]{0,2,1:T(8,128)(2,1)S(1)}, bf16[128,8,128]{0,2,1:T(8,128)(2,1)S(1)}, u32[]{:S(2)}, u32[]{:S(2)}) collective-permute-start(bf16[128,8,128]{0,2,1:T(8,128)(2,1)S(1)} %get-tuple-element.46), channel_id=1, source_target_pairs={{0,4},{4,8},{8,12},{12,16},{16,20},{20,24},{24,28},{28,32},{32,36}... | collective-permute-start | bytes 786440 | tf_op jit(solution)/shard_map/ppermute | solution.py:30
  178.7 1.3 copy.119
  180.0 5.8 %collective-permute-done.15 = bf16[128,8,128]{0,2,1:T(8,128)(2,1)S(1)} collective-permute-done((bf16[128,8,128]{0,2,1:T(8,128)(2,1)S(1)}, bf16[128,8,128]{0,2,1:T(8,128)(2,1)S(1)}, u32[]{:S(2)}, u32[]{:S(2)}) %collective-permute-start.15) | collective-permute-done | bytes 262176 | tf_op jit(solution)/shard_map/ppermute | solution.py:30
  (81 shorter events, 12.7 us)
Async XLA Ops:
  0.6 97.2 %copy-start = (bf16[512,1024]{1,0:T(8,128)(2,1)S(1)}, bf16[512,1024]{1,0:T(8,128)(2,1)}, u32[]{:S(2)}) copy-start(bf16[512,1024]{1,0:T(8,128)(2,1)} %param.9) | copy-start | bytes 3145732
  1.9 17.1 %collective-permute-start = (bf16[3,32,4096]{2,1,0:T(8,128)(2,1)S(1)}, bf16[3,32,4096]{2,1,0:T(8,128)(2,1)S(1)}, u32[]{:S(2)}, u32[]{:S(2)}) collective-permute-start(bf16[3,32,4096]{2,1,0:T(8,128)(2,1)S(1)} %pad_maximum_fusion.2), channel_id=1, source_target_pairs={{0,4},{4,8},{8,12},{12,16},{16,20},{20,24},{24,28},{28,32},{32,36}... | collective-permute-start | bytes 2359304 | tf_op jit(solution)/shard_map/ppermute | solution.py:21
  3.9 16.9 %collective-permute-start.1 = (bf16[3,32,4096]{2,1,0:T(8,128)(2,1)S(1)}, bf16[3,32,4096]{2,1,0:T(8,128)(2,1)S(1)}, u32[]{:S(2)}, u32[]{:S(2)}) collective-permute-start(bf16[3,32,4096]{2,1,0:T(8,128)(2,1)S(1)} %pad_maximum_fusion.2), channel_id=1, source_target_pairs={{4,0},{8,4},{12,8},{16,12},{20,16},{24,20},{28,24},{32,28},{36,32}... | collective-permute-start | bytes 2359304 | tf_op jit(solution)/shard_map/ppermute | solution.py:22
  22.1 6.3 %copy-start.16 = (s32[4]{0:T(128)S(1)}, s32[4]{0:T(128)}, u32[]{:S(2)}) copy-start(s32[4]{0:T(128)} %param.14) | copy-start | bytes 52
  22.1 6.3 %copy-start.17 = (s32[4]{0:T(128)S(1)}, s32[4]{0:T(128)}, u32[]{:S(2)}) copy-start(s32[4]{0:T(128)} %param.15) | copy-start | bytes 52
  24.0 32.0 %all-to-all-start = ((bf16[4,3,96,1024]{3,2,1,0:T(8,128)(2,1)}), bf16[4,3,96,1024]{3,2,1,0:T(8,128)(2,1)S(1)}, u32[]{:S(2)}, u32[]{:S(2)}) async-start(bf16[4,3,96,1024]{3,2,1,0:T(8,128)(2,1)} %pad_maximum_fusion.1), calls=%async_computation | async-start | bytes 4718592 | tf_op jit(solution)/shard_map/all_to_all | solution.py:55
  69.2 3.4 %copy-start.7 = (f32[8,512,384]{1,2,0:T(8,128)S(1)}, f32[8,512,384]{1,2,0:T(8,128)}, u32[]{:S(2)}) copy-start(f32[8,512,384]{1,2,0:T(8,128)} %get-tuple-element.55) | copy-start | bytes 18874372
  72.3 25.6 %copy-start.2 = (f32[8,384,512]{2,1,0:T(8,128)}, f32[8,384,512]{2,1,0:T(8,128)S(1)}, u32[]{:S(2)}) copy-start(f32[8,384,512]{2,1,0:T(8,128)S(1)} %get-tuple-element.57) | copy-start | bytes 18874372
  72.3 2.0 %copy-start.4 = (bf16[512,1024]{0,1:T(8,128)(2,1)S(1)}, bf16[512,1024]{0,1:T(8,128)(2,1)}, u32[]{:S(2)}) copy-start(bf16[512,1024]{0,1:T(8,128)(2,1)} %copy.102) | copy-start | bytes 3145732
  72.6 11.3 %copy-start.13 = (pred[48,8,4,128]{3,1,2,0:T(8,128)(4,1)S(1)}, pred[48,8,4,128]{3,1,2,0:T(8,128)(4,1)}, u32[]{:S(2)}) copy-start(pred[48,8,4,128]{3,1,2,0:T(8,128)(4,1)} %copy.152) | copy-start | bytes 589828
  77.5 80.9 %collective-permute-start.16 = (bf16[128,8,128]{0,2,1:T(8,128)(2,1)}, bf16[128,8,128]{0,2,1:T(8,128)(2,1)}, u32[]{:S(2)}, u32[]{:S(2)}) collective-permute-start(bf16[128,8,128]{0,2,1:T(8,128)(2,1)} %get-tuple-element.43), channel_id=1, source_target_pairs={{4,0},{8,4},{12,8},{16,12},{20,16},{24,20},{28,24},{32,28},{36,32}... | collective-permute-start | bytes 786440 | tf_op jit(solution)/shard_map/ppermute | solution.py:30
  86.0 27.0 %collective-permute-start.2 = (f32[8,128]{1,0:T(8,128)S(1)}, f32[8,128]{1,0:T(8,128)S(1)}, u32[]{:S(2)}, u32[]{:S(2)}) collective-permute-start(f32[8,128]{1,0:T(8,128)S(1)} %get-tuple-element.52), channel_id=1, source_target_pairs={{4,0},{8,4},{12,8},{16,12},{20,16},{24,20},{28,24},{32,28},{36,32}... | collective-permute-start | bytes 12296 | tf_op jit(solution)/shard_map/ppermute | solution.py:30
  87.9 27.0 %collective-permute-start.4 = (f32[8,128]{1,0:T(8,128)S(1)}, f32[8,128]{1,0:T(8,128)S(1)}, u32[]{:S(2)}, u32[]{:S(2)}) collective-permute-start(f32[8,128]{1,0:T(8,128)S(1)} %get-tuple-element.53), channel_id=1, source_target_pairs={{0,4},{4,8},{8,12},{12,16},{16,20},{20,24},{24,28},{28,32},{32,36}... | collective-permute-start | bytes 12296 | tf_op jit(solution)/shard_map/ppermute | solution.py:30
  90.3 30.4 %collective-permute-start.3 = (f32[8,128]{1,0:T(8,128)S(1)}, f32[8,128]{1,0:T(8,128)S(1)}, u32[]{:S(2)}, u32[]{:S(2)}) collective-permute-start(f32[8,128]{1,0:T(8,128)S(1)} %get-tuple-element.50), channel_id=1, source_target_pairs={{4,0},{8,4},{12,8},{16,12},{20,16},{24,20},{28,24},{32,28},{36,32}... | collective-permute-start | bytes 12296 | tf_op jit(solution)/shard_map/ppermute | solution.py:30
  95.6 7.4 %copy-start.9 = (bf16[1,3,4,32,1024]{4,3,1,2,0:T(8,128)(2,1)S(1)}, bf16[1,3,4,32,1024]{4,3,1,2,0:T(8,128)(2,1)}, u32[]{:S(2)}) copy-start(bf16[1,3,4,32,1024]{4,3,1,2,0:T(8,128)(2,1)} %get-tuple-element.36) | copy-start | bytes 2359300
  95.6 25.1 %collective-permute-start.5 = (f32[8,128]{1,0:T(8,128)S(1)}, f32[8,128]{1,0:T(8,128)S(1)}, u32[]{:S(2)}, u32[]{:S(2)}) collective-permute-start(f32[8,128]{1,0:T(8,128)S(1)} %get-tuple-element.51), channel_id=1, source_target_pairs={{0,4},{4,8},{8,12},{12,16},{16,20},{20,24},{24,28},{28,32},{32,36}... | collective-permute-start | bytes 12296 | tf_op jit(solution)/shard_map/ppermute | solution.py:30
  100.0 4.0 %copy-start.15 = (f32[384,8,128]{0,2,1:T(8,128)}, f32[384,8,128]{0,2,1:T(8,128)S(1)}, u32[]{:S(2)}) copy-start(f32[384,8,128]{0,2,1:T(8,128)S(1)} %fusion.30) | copy-start | bytes 4718596
  101.3 2.7 %copy-start.8 = (bf16[1,3,4,32,1024]{4,3,1,2,0:T(8,128)(2,1)S(1)}, bf16[1,3,4,32,1024]{4,3,1,2,0:T(8,128)(2,1)}, u32[]{:S(2)}) copy-start(bf16[1,3,4,32,1024]{4,3,1,2,0:T(8,128)(2,1)} %get-tuple-element.34) | copy-start | bytes 2359300
  103.2 1.1 copy-start.10
  105.6 32.5 %copy-start.12 = (bf16[384,8,128]{0,2,1:T(8,128)(2,1)S(1)}, bf16[384,8,128]{0,2,1:T(8,128)(2,1)}, u32[]{:S(2)}) copy-start(bf16[384,8,128]{0,2,1:T(8,128)(2,1)} %copy.112) | copy-start | bytes 2359300
  113.0 45.4 %collective-permute-start.17 = (bf16[128,8,128]{0,2,1:T(8,128)(2,1)}, bf16[128,8,128]{0,2,1:T(8,128)(2,1)}, u32[]{:S(2)}, u32[]{:S(2)}) collective-permute-start(bf16[128,8,128]{0,2,1:T(8,128)(2,1)} %get-tuple-element.44), channel_id=1, source_target_pairs={{0,4},{4,8},{8,12},{12,16},{16,20},{20,24},{24,28},{28,32},{32,36}... | collective-permute-start | bytes 786440 | tf_op jit(solution)/shard_map/ppermute | solution.py:30
  114.9 31.9 %collective-permute-start.6 = (f32[128,8,128]{0,2,1:T(8,128)}, f32[128,8,128]{0,2,1:T(8,128)}, u32[]{:S(2)}, u32[]{:S(2)}) collective-permute-start(f32[128,8,128]{0,2,1:T(8,128)} %get-tuple-element.41), channel_id=1, source_target_pairs={{4,0},{8,4},{12,8},{16,12},{20,16},{24,20},{28,24},{32,28},{36,32}... | collective-permute-start | bytes 1572872 | tf_op jit(solution)/shard_map/ppermute | solution.py:30
  120.7 7.7 %collective-permute-start.8 = (f32[8,128]{1,0:T(8,128)S(1)}, f32[8,128]{1,0:T(8,128)S(1)}, u32[]{:S(2)}, u32[]{:S(2)}) collective-permute-start(f32[8,128]{1,0:T(8,128)S(1)} %get-tuple-element.33), channel_id=1, source_target_pairs={{0,4},{4,8},{8,12},{12,16},{16,20},{20,24},{24,28},{28,32},{32,36}... | collective-permute-start | bytes 12296 | tf_op jit(solution)/shard_map/ppermute | solution.py:21
  122.7 7.7 %collective-permute-start.9 = (f32[8,128]{1,0:T(8,128)S(1)}, f32[8,128]{1,0:T(8,128)S(1)}, u32[]{:S(2)}, u32[]{:S(2)}) collective-permute-start(f32[8,128]{1,0:T(8,128)S(1)} %get-tuple-element.33), channel_id=1, source_target_pairs={{4,0},{8,4},{12,8},{16,12},{20,16},{24,20},{28,24},{32,28},{36,32}... | collective-permute-start | bytes 12296 | tf_op jit(solution)/shard_map/ppermute | solution.py:22
  128.4 7.7 %collective-permute-start.10 = (f32[8,128]{1,0:T(8,128)S(1)}, f32[8,128]{1,0:T(8,128)S(1)}, u32[]{:S(2)}, u32[]{:S(2)}) collective-permute-start(f32[8,128]{1,0:T(8,128)S(1)} %get-tuple-element.48), channel_id=1, source_target_pairs={{0,4},{4,8},{8,12},{12,16},{16,20},{20,24},{24,28},{28,32},{32,36}... | collective-permute-start | bytes 12296 | tf_op jit(solution)/shard_map/ppermute | solution.py:21
  130.4 7.7 %collective-permute-start.11 = (f32[8,128]{1,0:T(8,128)S(1)}, f32[8,128]{1,0:T(8,128)S(1)}, u32[]{:S(2)}, u32[]{:S(2)}) collective-permute-start(f32[8,128]{1,0:T(8,128)S(1)} %get-tuple-element.48), channel_id=1, source_target_pairs={{4,0},{8,4},{12,8},{16,12},{20,16},{24,20},{28,24},{32,28},{36,32}... | collective-permute-start | bytes 12296 | tf_op jit(solution)/shard_map/ppermute | solution.py:22
  136.2 12.9 %collective-permute-start.7 = (f32[128,8,128]{0,2,1:T(8,128)}, f32[128,8,128]{0,2,1:T(8,128)}, u32[]{:S(2)}, u32[]{:S(2)}) collective-permute-start(f32[128,8,128]{0,2,1:T(8,128)} %get-tuple-element.42), channel_id=1, source_target_pairs={{0,4},{4,8},{8,12},{12,16},{16,20},{20,24},{24,28},{28,32},{32,36}... | collective-permute-start | bytes 1572872 | tf_op jit(solution)/shard_map/ppermute | solution.py:30
  144.4 17.0 %copy-start.5 = (bf16[512,1024]{0,1:T(8,128)(2,1)S(1)}, bf16[512,1024]{0,1:T(8,128)(2,1)}, u32[]{:S(2)}) copy-start(bf16[512,1024]{0,1:T(8,128)(2,1)} %copy.102) | copy-start | bytes 3145732
  144.4 17.0 %copy-start.11 = (bf16[48,8,8,128]{3,2,1,0:T(8,128)(2,1)S(1)}, bf16[48,8,8,128]{3,2,1,0:T(8,128)(2,1)}, u32[]{:S(2)}) copy-start(bf16[48,8,8,128]{3,2,1,0:T(8,128)(2,1)} %copy-done.10) | copy-start | bytes 2359300
  144.4 17.0 %copy-start.14 = (pred[48,8,4,128]{3,1,2,0:T(8,128)(4,1)S(1)}, pred[48,8,4,128]{3,1,2,0:T(8,128)(4,1)}, u32[]{:S(2)}) copy-start(pred[48,8,4,128]{3,1,2,0:T(8,128)(4,1)} %copy.152) | copy-start | bytes 589828
  150.7 10.7 %collective-permute-start.12 = (f32[8,128]{1,0:T(8,128)S(1)}, f32[8,128]{1,0:T(8,128)S(1)}, u32[]{:S(2)}, u32[]{:S(2)}) collective-permute-start(f32[8,128]{1,0:T(8,128)S(1)} %bitcast.184), channel_id=1, source_target_pairs={{0,4},{4,8},{8,12},{12,16},{16,20},{20,24},{24,28},{28,32},{32,36}... | collective-permute-start | bytes 12296 | tf_op jit(solution)/shard_map/ppermute | solution.py:21
  152.6 8.8 %collective-permute-start.13 = (f32[8,128]{1,0:T(8,128)S(1)}, f32[8,128]{1,0:T(8,128)S(1)}, u32[]{:S(2)}, u32[]{:S(2)}) collective-permute-start(f32[8,128]{1,0:T(8,128)S(1)} %bitcast.185), channel_id=1, source_target_pairs={{4,0},{8,4},{12,8},{16,12},{20,16},{24,20},{28,24},{32,28},{36,32}... | collective-permute-start | bytes 12296 | tf_op jit(solution)/shard_map/ppermute | solution.py:22
  161.4 8.3 %copy-start.3 = (bf16[512,1024]{0,1:T(8,128)(2,1)S(1)}, bf16[512,1024]{0,1:T(8,128)(2,1)}, u32[]{:S(2)}) copy-start(bf16[512,1024]{0,1:T(8,128)(2,1)} %copy.131) | copy-start | bytes 3145732
  169.7 8.3 %copy-start.6 = (bf16[384,8,128]{0,2,1:T(8,128)(2,1)S(1)}, bf16[384,8,128]{0,2,1:T(8,128)(2,1)}, u32[]{:S(2)}) copy-start(bf16[384,8,128]{0,2,1:T(8,128)(2,1)} %copy.110) | copy-start | bytes 2359300
  169.7 18.2 %copy-start.1 = (bf16[512,1024]{1,0:T(8,128)(2,1)S(1)}, bf16[512,1024]{1,0:T(8,128)(2,1)}, u32[]{:S(2)}) copy-start(bf16[512,1024]{1,0:T(8,128)(2,1)} %param.9) | copy-start | bytes 3145732
  172.0 8.0 %collective-permute-start.14 = (bf16[128,8,128]{0,2,1:T(8,128)(2,1)S(1)}, bf16[128,8,128]{0,2,1:T(8,128)(2,1)S(1)}, u32[]{:S(2)}, u32[]{:S(2)}) collective-permute-start(bf16[128,8,128]{0,2,1:T(8,128)(2,1)S(1)} %get-tuple-element.45), channel_id=1, source_target_pairs={{4,0},{8,4},{12,8},{16,12},{20,16},{24,20},{28,24},{32,28},{36,32}... | collective-permute-start | bytes 786440 | tf_op jit(solution)/shard_map/ppermute | solution.py:30
  176.0 9.8 %collective-permute-start.15 = (bf16[128,8,128]{0,2,1:T(8,128)(2,1)S(1)}, bf16[128,8,128]{0,2,1:T(8,128)(2,1)S(1)}, u32[]{:S(2)}, u32[]{:S(2)}) collective-permute-start(bf16[128,8,128]{0,2,1:T(8,128)(2,1)S(1)} %get-tuple-element.46), channel_id=1, source_target_pairs={{0,4},{4,8},{8,12},{12,16},{16,20},{20,24},{24,28},{28,32},{32,36}... | collective-permute-start | bytes 786440 | tf_op jit(solution)/shard_map/ppermute | solution.py:30
